TPU v7x, 32 devices: a whole 2x2x4 slice. The times are simulated.
32 devices in a mesh: arc: 2 (over y), trow: 4 (over z), tcol: 4 (over x, core).
Axes of the slice: x: 2, y: 2, z: 4, core: 2. Of those that a mesh axis runs over, the one named last changes fastest.
Arguments:
- design: bfloat16 [1280, 8192], P('arc', 'tcol'), may hold values from -0.25 to 0.25
- local_design: bfloat16 [1280, 128], P('arc'), may hold values from -0.3125 to 0.3125
- lengths: int32 [4], P('arc'), may hold values from 1 to 320, 960 in all
- regularizer: float32 [8192], P(('arc', 'trow')), may hold values from 0.2 to 2
Outputs:
- normal: float32 [8192, 8192], P(('arc', 'trow'), 'tcol')
- panel_factor: float32 [2, 8192, 512], P(None, 'tcol')
Inputs may be any that keep to these rules, and one draw needn't show every extreme that they name: `lengths`: each arc has at least one live row; some arc is full.
All inputs are finite; a program needn't handle non-finite values. No bound on the sum of `lengths` on one device may be relied on, other than what follows from the above.
Results may differ from a plain program's by a relative error of at most 0.003.
Values may be sent and summed in bfloat16 or wider, within the bound.
No kernel may reach another device: no remote copies, remote signals or barrier semaphores. Data moves between devices by JAX's collectives and lax.ppermute only.
A program may use at most 128 MiB of HBM per device.

v0:
```python
import functools

import jax
import jax.numpy as jnp
from jax import lax
from jax.experimental import pallas as pl
from jax.experimental.pallas import tpu as pltpu
from jax.sharding import PartitionSpec as P

PANEL = 512
PANELS = 2
AXES = ("arc", "trow", "tcol")
CORES = 2


ridge = 0.1

HIGHEST = lax.Precision.HIGHEST
LANES = 128
CHUNK = 512
SUB = 8


def inverse_factor(rows):
    groups = LANES // SUB
    rows = list(rows)
    lane = lax.broadcasted_iota(jnp.int32, (SUB, LANES), 1)
    sub = lax.broadcasted_iota(jnp.int32, (SUB, LANES), 0)
    shape = (SUB, LANES)
    out = []
    for s in range(groups):
        j = s * SUB
        inside = (lane >= j) & (lane < j + SUB)
        lead = rows[s]
        merged = jnp.where(inside, jnp.where(lane == sub + j, 1.0, 0.0), lead)
        z = [jnp.broadcast_to(merged[k : k + 1, :], shape) for k in range(SUB)]
        sp = {
            (m, k): jnp.broadcast_to(lead[k : k + 1, j + m : j + m + 1], shape)
            for k in range(SUB)
            for m in range(k, SUB)
        }
        below = range(s + 1, groups)
        col = {
            (t, k): jnp.broadcast_to(rows[t][:, j + k : j + k + 1], shape)
            for t in below
            for k in range(SUB)
        }
        rest = {t: jnp.where(inside, 0.0, rows[t]) for t in below}
        for k in range(0, SUB, 2):
            a, b, c = sp[k, k], sp[k + 1, k], sp[k + 1, k + 1]
            det = a * c - b * b
            root = lax.rsqrt(det)
            scale = root * root
            pair = {
                m: (c * sp[m, k] - b * sp[m, k + 1], a * sp[m, k + 1] - b * sp[m, k])
                for m in range(k + 2, SUB)
            }
            first = lax.rsqrt(a)
            second = root * (a * first)
            one = {m: sp[m, k] * first for m in range(k + 1, SUB)}
            two = {m: (sp[m, k + 1] - one[k + 1] * one[m]) * second for m in range(k + 2, SUB)}
            for m in range(k + 2, SUB):
                for n in range(m, SUB):
                    sp[n, m] = sp[n, m] - (sp[n, k] * pair[m][0] + sp[n, k + 1] * pair[m][1]) * scale
            for at, inv, l in ((k, first, one), (k + 1, second, two)):
                z[at] = z[at] * inv
                for m in range(at + 1, SUB):
                    z[m] = z[m] - l[m] * z[at]
                for t in below:
                    coef = col[t, at] * inv
                    for m in range(at + 1, SUB):
                        col[t, m] = col[t, m] - coef * l[m]
                    rest[t] = rest[t] - coef * z[at]
        for t in below:
            rows[t] = rest[t]
        done = z[0]
        for k in range(1, SUB):
            done = jnp.where(sub == k, z[k], done)
        out.append(jnp.where(lane <= sub + j, done, 0.0))
    return out


def rows_of(block):
    return [block[SUB * t:SUB * (t + 1), :] for t in range(LANES // SUB)]


class Plan:
    def __init__(self, mesh):
        self.arc, self.trow, self.tcol = (mesh.shape[name] for name in AXES)
        self.across = self.tcol // CORES

    def flat(self, arc, trow, tcol):
        return (arc % self.arc * self.trow + trow) * self.tcol + tcol % self.tcol

    def move(self, block, arcs, across, source=None):
        pairs = [
            (self.flat(a, r, c), self.flat(a + arcs, r, c + across * CORES))
            for a in range(self.arc)
            for r in range(self.trow)
            for c in range(self.tcol)
            if source is None or source(a, r, c)
        ]
        return lax.ppermute(block, AXES, pairs)

    def core_swap(self, block):
        pairs = [
            (self.flat(a, r, c), self.flat(a, r, c ^ 1))
            for a in range(self.arc)
            for r in range(self.trow)
            for c in range(self.tcol)
        ]
        return lax.ppermute(block, AXES, pairs)

    def own_half(self, block, holder_core):
        half = block.shape[0] // CORES
        core = lax.axis_index("tcol") % CORES
        got = self.core_swap(block)
        mine = lax.dynamic_slice_in_dim(block, core * half, half, 0)
        theirs = lax.dynamic_slice_in_dim(got, core * half, half, 0)
        return jnp.where(core == holder_core, mine, theirs)

    def gather_rows(self, tile):
        me = lax.axis_index("arc") * self.trow + lax.axis_index("trow")
        total = self.arc * self.trow
        spans = [self.trow << n for n in range(self.arc.bit_length() - 1)]
        spans += [1 << n for n in range(self.trow.bit_length() - 1)]
        tile = tile[None]
        for span in spans:
            pairs = [
                (t * self.tcol + c, (t ^ span) * self.tcol + c)
                for t in range(total)
                for c in range(self.tcol)
            ]
            got = lax.ppermute(tile, AXES, pairs)
            low = (me & span) == 0
            tile = jnp.concatenate([jnp.where(low, tile, got), jnp.where(low, got, tile)])
        blocks = tile.reshape(self.trow, self.arc, -1)
        return jnp.transpose(blocks, (1, 0, 2)).reshape(-1)


def local_kernel(a_ref, n_ref):
    n_ref[0] = jnp.concatenate(inverse_factor(rows_of(a_ref[0])), axis=0)


def local_call(a):
    block = pl.BlockSpec((1,) + a.shape[1:], lambda i: (i, 0, 0))
    return pl.pallas_call(
        local_kernel,
        out_shape=jax.ShapeDtypeStruct(a.shape, jnp.float32),
        grid=(a.shape[0],),
        in_specs=[block],
        out_specs=block,
        name="local_inverse",
    )(a)


def local_basis(local_half):
    local_normal = jnp.einsum(
        "acl,acm->alm", local_half, local_half, preferred_element_type=jnp.float32
    )
    local_normal = local_normal + ridge * jnp.eye(local_half.shape[2], dtype=jnp.float32)[None]
    inverse = local_call(local_normal)
    basis_rows = jnp.einsum(
        "alm,acm->alc", inverse, local_half.astype(jnp.float32), precision=HIGHEST
    )
    return basis_rows.astype(jnp.bfloat16)


def after(value, *earlier):
    return lax.optimization_barrier((value,) + earlier)[0]


def product(left, right, dims, precision=None):
    return lax.dot_general(
        left, right, (dims, ((), ())), precision=precision, preferred_element_type=jnp.float32
    )


def fine(left, right, dims):
    left_top, right_top = left.astype(jnp.bfloat16), right.astype(jnp.bfloat16)
    left_rest = (left - left_top.astype(jnp.float32)).astype(jnp.bfloat16)
    right_rest = (right - right_top.astype(jnp.float32)).astype(jnp.bfloat16)
    return product(left_top, right_top, dims) + (
        product(left_top, right_rest, dims) + product(left_rest, right_top, dims)
    )


def eliminate(m_ref):
    n = m_ref.shape[0]
    blocks = n // LANES
    row = lax.broadcasted_iota(jnp.int32, (LANES, LANES), 0)
    col = lax.broadcasted_iota(jnp.int32, (LANES, LANES), 1)

    def step(i, carry):
        at = pl.ds(pl.multiple_of(i * LANES, LANES), LANES)
        inv = jnp.concatenate(inverse_factor(rows_of(m_ref[at, at])), axis=0)
        m_ref[at, at] = jnp.where(row == col, 1.0, 0.0)
        m_ref[at, :] = fine(inv, m_ref[at, :], ((1,), (0,)))

        def update(t, carry):
            to = pl.ds(pl.multiple_of(t * LANES, LANES), LANES)
            coef = m_ref[at, to]
            m_ref[to, at] = jnp.zeros((LANES, LANES), jnp.float32)
            m_ref[to, :] = m_ref[to, :] - fine(coef, m_ref[at, :], ((0,), (0,)))
            return carry

        lax.fori_loop(i + 1, blocks, update, 0)
        kept = lax.broadcasted_iota(jnp.int32, (LANES, n), 1) < (i + 1) * LANES
        m_ref[at, :] = jnp.where(kept, m_ref[at, :], 0.0)
        return carry

    lax.fori_loop(0, blocks, step, 0)


def on_diagonal(values, n):
    row = lax.broadcasted_iota(jnp.int32, (n, n), 0)
    col = lax.broadcasted_iota(jnp.int32, (n, n), 1)
    return jnp.where(row == col, values, 0.0)


def clean(block, basis, turned):
    loadings = product(basis, block, ((1,), (0,))).astype(jnp.bfloat16)
    return (block.astype(jnp.float32) - product(turned, loadings, ((1,), (0,)))).astype(
        jnp.bfloat16
    )


def clean_pieces(choices, layout, table_ref, base, basis_ref, turned_ref, out_ref):
    capacity = basis_ref.shape[2]
    for n, (candidates, at) in enumerate(layout):
        slot, rel, chosen = (table_ref[base + 3 * n + i] for i in range(3))
        to = pl.ds(pl.multiple_of(slot * capacity, 64), capacity)
        rows = slice(at * capacity, (at + 1) * capacity)

        def put(ref, to=to, rows=rows, rel=rel):
            out_ref[to, :] = clean(ref[rows, :], basis_ref[rel], turned_ref[rel])

        if len(candidates) == 1:
            put(choices[candidates[0]])
            continue
        for which, candidate in enumerate(candidates):

            @pl.when(chosen == which)
            def _(put=put, candidate=candidate):
                put(choices[candidate])


def turn_bases(moved_refs, basis_ref, turned_ref):
    for s, moved in enumerate(moved_refs):
        for a in range(moved.shape[0]):
            basis_ref[s * moved.shape[0] + a] = moved[a]
            turned_ref[s * moved.shape[0] + a] = moved[a].T


def split(value):
    top = value.astype(jnp.bfloat16)
    return top, (value - top.astype(jnp.float32)).astype(jnp.bfloat16)


def weigh(terms, top_ref, rest_ref):
    rows = top_ref.shape[0]
    chunk = next(n for n in (512, 320, 256, LANES, SUB) if rows % n == 0 and rows > n)
    parts = [(ref, *split(factor)) for ref, factor in terms]

    def step(i, carry):
        at = pl.ds(pl.multiple_of(i * chunk, chunk), chunk)
        total = None
        for ref, top, rest in parts:
            x = ref[at, :]
            term = product(x, top, ((1,), (1,))) + product(x, rest, ((1,), (1,)))
            total = term if total is None else total + term
        top_ref[at, :], rest_ref[at, :] = split(total)
        return carry

    lax.fori_loop(0, rows // chunk, step, 0)


def first_kernel(arcs, pieces, layout, table_ref, d_ref, *refs):
    moved, refs = refs[:arcs], refs[arcs:]
    piece_refs = refs[:pieces]
    x_ref, m_ref, top_ref, rest_ref, md_ref, basis_ref, turned_ref = refs[pieces:]
    turn_bases(moved, basis_ref, turned_ref)
    n = m_ref.shape[0]
    clean_pieces(piece_refs, layout, table_ref, 0, basis_ref, turned_ref, x_ref)
    x = x_ref[...]
    m_ref[...] = product(x, x, ((0,), (0,))) + on_diagonal(d_ref[...], n)
    eliminate(m_ref)
    inverse = m_ref[...]
    weigh([(x_ref, inverse)], top_ref, rest_ref)
    md_ref[...] = (inverse * d_ref[...]).T


def next_kernel(arcs, pieces, layout, table_ref, d_ref, *refs):
    moved, refs = refs[:arcs], refs[arcs:]
    piece_refs, refs = refs[:pieces], refs[pieces:]
    before_ref, prior_ref, top_ref, rest_ref, md_ref = refs[:5]
    basis_ref, turned_ref, x_ref, m_ref, cross_ref = refs[5:]
    turn_bases(moved, basis_ref, turned_ref)
    n = m_ref.shape[0]
    clean_pieces(piece_refs, layout, table_ref, 0, basis_ref, turned_ref, x_ref)
    x = x_ref[...]
    cross = fine(prior_ref[...], product(before_ref[...], x, ((0,), (0,))), ((1,), (0,)))
    m_ref[...] = product(x, x, ((0,), (0,))) + on_diagonal(d_ref[...], n) - fine(
        cross, cross, ((0,), (0,))
    )
    cross_ref[...] = fine(cross, prior_ref[...], ((0,), (0,)))
    eliminate(m_ref)
    inverse = m_ref[...]
    back = -fine(inverse, cross_ref[...], ((1,), (0,)))
    weigh([(x_ref, inverse), (before_ref, back)], top_ref, rest_ref)
    md_ref[...] = (inverse * d_ref[...]).T


def pivot_call(panel, layout, table, values, basis, pieces, prior):
    own_arcs, local, capacity = basis[0].shape
    rows = own_arcs * len(basis) * capacity
    square = jax.ShapeDtypeStruct((PANEL, PANEL), jnp.float32)
    tall = jax.ShapeDtypeStruct((rows, PANEL), jnp.bfloat16)
    vmem = pl.BlockSpec(memory_space=pltpu.VMEM)
    kernel, outs, scratch, _ = (
        (first_kernel, [tall, square, tall, tall, square], [], "pivot_first")
        if panel == 0
        else (
            next_kernel,
            [tall, tall, square],
            [
                pltpu.VMEM((rows, PANEL), jnp.bfloat16),
                pltpu.VMEM((PANEL, PANEL), jnp.float32),
                pltpu.VMEM((PANEL, PANEL), jnp.float32),
            ],
            "pivot_next",
        )
    )
    scratch = [
        pltpu.VMEM((own_arcs * len(basis), local, capacity), jnp.bfloat16),
        pltpu.VMEM((own_arcs * len(basis), capacity, local), jnp.bfloat16),
    ] + scratch
    args = (values[None, :], *basis, *pieces, *prior)
    return pl.pallas_call(
        functools.partial(kernel, len(basis), len(pieces), layout),
        out_shape=outs,
        in_specs=[pl.BlockSpec(memory_space=pltpu.SMEM)] + [vmem] * len(args),
        out_specs=[vmem] * len(outs),
        scratch_shapes=scratch,
        compiler_params=pltpu.CompilerParams(vmem_limit_bytes=56 << 20),
    )(table, *args)


def assemble_kernel(spec, table_ref, own_ref, *refs):
    arcs, own_arcs, pieces, layout = spec
    got_refs, refs = refs[: arcs - 1], refs[arcs - 1 :]
    tile_refs, refs = refs[:pieces], refs[pieces:]
    moved, refs = refs[:arcs], refs[arcs:]
    top0, top1, rest0, rest1, md0, md1, d_ref, normal_ref, panel_ref = refs[:9]
    basis_ref, turned_ref, xc, xct, xr, xrt, fr_top, fr_rest, fc_top, fc_rest, work = refs[9:]
    width, tile_rows = xc.shape[1], xr.shape[1]
    total_rows = xc.shape[0]
    row_start = table_ref[0]
    tile_start = table_ref[1] + pl.program_id(0) * width
    chunk = min(CHUNK, tile_rows, width)

    def turn(source, target):
        for at in range(0, total_rows, LANES):
            target[:, at : at + LANES] = source[at : at + LANES, :].T

    def factor(xt_ref, at, start):
        xt = xt_ref[at, :]
        for panel, (top, rest) in enumerate(((top0, rest0), (top1, rest1))):
            to = slice(panel * PANEL, (panel + 1) * PANEL)
            work[:, to] = product(xt, top[...], ((1,), (0,))) + product(xt, rest[...], ((1,), (0,)))
        for panel, md in enumerate((md0, md1)):
            to = slice(panel * PANEL, (panel + 1) * PANEL)

            @pl.when((start >= panel * PANEL) & (start < (panel + 1) * PANEL))
            def _(to=to, md=md, panel=panel):
                off = pl.multiple_of(start - panel * PANEL, chunk)
                work[:, to] = work[:, to] + md[pl.ds(off, chunk), :]

            @pl.when(start < panel * PANEL)
            def _(to=to):
                work[:, to] = jnp.zeros((chunk, PANEL), jnp.float32)

    @pl.when(pl.program_id(0) == 0)
    def _():
        turn_bases(moved, basis_ref, turned_ref)
        clean_pieces(tile_refs, layout, table_ref, 2, basis_ref, turned_ref, xr)
        turn(xr, xrt)

        def row_chunk(i, carry):
            at = pl.ds(pl.multiple_of(i * chunk, chunk), chunk)
            factor(xrt, at, row_start + i * chunk)
            fr_top[at, :], fr_rest[at, :] = split(work[...])
            return carry

        lax.fori_loop(0, tile_rows // chunk, row_chunk, 0)

    columns = [((s,), a) for s in range(arcs) for a in range(own_arcs)]
    clean_pieces(
        [own_ref, *got_refs], columns, table_ref, 2 + 3 * len(layout), basis_ref, turned_ref, xc
    )
    turn(xc, xct)

    def col_chunk(i, carry):
        at = pl.ds(pl.multiple_of(i * chunk, chunk), chunk)
        factor(xct, at, tile_start + i * chunk)
        for panel in range(PANELS):
            panel_ref[panel, at, :] = work[:, panel * PANEL : (panel + 1) * PANEL]
        fc_top[at, :], fc_rest[at, :] = split(work[...])
        return carry

    lax.fori_loop(0, width // chunk, col_chunk, 0)
    d = d_ref[:, pl.ds(pl.multiple_of(jnp.clip(tile_start - row_start, 0, tile_rows - width), LANES), width)]

    def normal_chunk(i, carry):
        at = pl.ds(pl.multiple_of(i * chunk, chunk), chunk)
        dims = ((1,), (1,))
        value = product(xrt[at, :], xc[...], ((1,), (0,))) - (
            product(fr_top[at, :], fc_top[...], dims)
            + (product(fr_top[at, :], fc_rest[...], dims) + product(fr_rest[at, :], fc_top[...], dims))
        )
        row = lax.broadcasted_iota(jnp.int32, (chunk, width), 0) + (row_start + i * chunk)
        col = lax.broadcasted_iota(jnp.int32, (chunk, width), 1) + tile_start
        normal_ref[at, :] = value + jnp.where(row == col, d, 0.0)
        return carry

    lax.fori_loop(0, tile_rows // chunk, normal_chunk, 0)


def assemble(own, got, tiles, layout, basis, tops, rests, mds, regularizer, table, own_arcs):
    arcs = len(got) + 1
    rows = own.shape[0] * arcs
    col_width, tile_rows = own.shape[1], regularizer.shape[0]
    width = min(512 if rows <= 2048 else 256, col_width, tile_rows)
    depth = PANEL * PANELS
    chunk = min(CHUNK, tile_rows, width)
    once = pl.Buffered(1)

    def whole(array):
        zeros = (0,) * array.ndim
        return pl.BlockSpec(array.shape, lambda s, t: zeros, pipeline_mode=once)

    fixed = [*tiles, *basis, *tops, *rests, *mds, regularizer[None, :]]
    columns = pl.BlockSpec((own.shape[0], width), lambda s, t: (0, s))
    return pl.pallas_call(
        functools.partial(assemble_kernel, (arcs, own_arcs, len(tiles), layout)),
        out_shape=(
            jax.ShapeDtypeStruct((tile_rows, col_width), jnp.float32),
            jax.ShapeDtypeStruct((PANELS, col_width, PANEL), jnp.float32),
        ),
        grid_spec=pltpu.PrefetchScalarGridSpec(
            num_scalar_prefetch=1,
            grid=(col_width // width,),
            in_specs=[columns] * arcs + [whole(array) for array in fixed],
            out_specs=(
                pl.BlockSpec((tile_rows, width), lambda s, t: (0, s)),
                pl.BlockSpec((PANELS, width, PANEL), lambda s, t: (0, s, 0)),
            ),
            scratch_shapes=[
                pltpu.VMEM((own_arcs * arcs, *basis[0].shape[1:]), jnp.bfloat16),
                pltpu.VMEM((own_arcs * arcs, *basis[0].shape[:0:-1]), jnp.bfloat16),
                pltpu.VMEM((rows, width), jnp.bfloat16),
                pltpu.VMEM((width, rows), jnp.bfloat16),
                pltpu.VMEM((rows, tile_rows), jnp.bfloat16),
                pltpu.VMEM((tile_rows, rows), jnp.bfloat16),
                pltpu.VMEM((tile_rows, depth), jnp.bfloat16),
                pltpu.VMEM((tile_rows, depth), jnp.bfloat16),
                pltpu.VMEM((width, depth), jnp.bfloat16),
                pltpu.VMEM((width, depth), jnp.bfloat16),
                pltpu.VMEM((chunk, depth), jnp.float32),
            ],
        ),
        compiler_params=pltpu.CompilerParams(vmem_limit_bytes=60 << 20),
        name="assemble",
    )(table, own, *got, *fixed)


def per_device(plan, design, local_design, lengths, regularizer):
    row_count, col_width = design.shape
    tile_rows = regularizer.shape[0]
    own_arcs = lengths.shape[0]
    capacity = row_count // own_arcs
    half_arcs = own_arcs // CORES
    arc_index, trow_index = lax.axis_index("arc"), lax.axis_index("trow")
    tcol_index = lax.axis_index("tcol")
    core, x_index = tcol_index % CORES, tcol_index // CORES
    row_start = (arc_index * plan.trow + trow_index) * tile_rows
    col_start = tcol_index * col_width
    lead = PANEL * PANELS

    live_rows = jnp.arange(capacity, dtype=jnp.int32)[None, :] < lengths[:, None]
    live_flat = live_rows.reshape(row_count, 1)
    zero = jnp.zeros((), design.dtype)

    def arc_back(s):
        return lax.rem(arc_index + plan.arc - s, plan.arc)

    def half_entries(halves_count):
        layout, entries = [], []
        for n, which in enumerate((core, 1 - core)):
            for s in range(plan.arc):
                for a in range(half_arcs):
                    offset = which * half_arcs + a
                    layout.append(((n * halves_count + s,), a))
                    entries += [arc_back(s) * own_arcs + offset, s * own_arcs + offset, 0]
        return layout, entries

    def from_lead(arc, trow, tcol):
        return tcol < CORES

    def spread_lead(mine, source):
        return [
            [
                plan.move(mine, s, dx, source) if s or dx else mine
                for dx in range(plan.across)
            ]
            for s in range(plan.arc)
        ]

    def lead_block(panel, live):
        return jnp.where(live, design[:, panel * PANEL : (panel + 1) * PANEL], zero)

    mine = plan.own_half(lead_block(0, live_flat), 0)
    halves = []
    for arrived in spread_lead(mine, None):
        best = arrived[0]
        for dx in range(1, plan.across):
            best = jnp.where(x_index == dx, arrived[dx], best)
        halves.append(best)
    first_pieces = halves + [plan.core_swap(half) for half in halves]

    live_rows, local_design = lax.optimization_barrier((live_rows, local_design, mine))[:2]
    local_half = local_design.reshape(own_arcs, capacity, -1)
    local_half = jnp.where(live_rows[:, :, None], local_half, jnp.zeros((), local_design.dtype))
    basis_own = local_basis(local_half)
    basis = [basis_own] + [plan.move(basis_own, s, 0) for s in range(1, plan.arc)]

    live_flat = after(live_flat, basis_own)
    block = lead_block(1, live_flat)
    mine = jnp.where(core == 0, block, plan.core_swap(block))
    arrivals = spread_lead(mine, from_lead)
    next_pieces = [got for arrived in arrivals for got in arrived]
    next_layout = [
        (tuple(s * plan.across + dx for dx in range(plan.across)), a)
        for s in range(plan.arc)
        for a in range(own_arcs)
    ]
    live_flat = after(live_flat, mine)

    masked = jnp.where(live_flat, design, zero)
    got_columns = [plan.move(masked, s, 0) for s in range(1, plan.arc)]

    def holder(a, r):
        return (a % plan.arc * plan.trow + r) * tile_rows // col_width

    my_holder = row_start // col_width
    halves = []
    for s in range(plan.arc):
        target = (lax.rem(arc_index + s, plan.arc) * plan.trow + trow_index) * tile_rows
        tile = lax.dynamic_slice_in_dim(masked, lax.rem(target, col_width), tile_rows, 1)
        mine = plan.own_half(tile, target // col_width % CORES)

        def has_tile(a, r, c, s=s):
            return holder(a + s, r) // CORES == c // CORES

        arrived = [
            plan.move(mine, s, dx, has_tile if s else None) if s or dx else mine
            for dx in range(plan.across)
        ]
        best = arrived[0]
        for dx in range(1, plan.across):
            far = lax.rem(x_index + plan.across - my_holder // CORES, plan.across) == dx
            best = jnp.where(far, arrived[dx], best)
        halves.append(best)

    lead_tiles = -(-lead // tile_rows)
    all_regularizer = plan.gather_rows(regularizer)[: lead_tiles * tile_rows][:lead]

    def table_of(*values):
        return jnp.stack([jnp.asarray(v, jnp.int32) for v in values])

    layout, entries = half_entries(plan.arc)
    first_rows, prior, *first_parts = pivot_call(
        0, layout, table_of(*entries), all_regularizer[:PANEL], basis, first_pieces, ()
    )

    def arc_entries(chosen):
        return [
            v
            for s in range(plan.arc)
            for a in range(own_arcs)
            for v in (arc_back(s) * own_arcs + a, s * own_arcs + a, chosen)
        ]

    next_parts = pivot_call(
        1,
        next_layout,
        table_of(*arc_entries(x_index)),
        all_regularizer[PANEL:lead],
        basis,
        next_pieces,
        (first_rows, prior),
    )
    tiles = halves + [plan.core_swap(half) for half in halves]
    return assemble(
        masked,
        got_columns,
        tiles,
        layout,
        basis,
        *[[a, b] for a, b in zip(first_parts, next_parts)],
        regularizer,
        table_of(row_start, col_start, *entries, *arc_entries(0)),
        own_arcs,
    )


def solution(mesh):
    plan = Plan(mesh)

    def body(*args):
        return per_device(plan, *args)

    return jax.shard_map(
        body,
        mesh=mesh,
        in_specs=(P("arc", "tcol"), P("arc", None), P("arc"), P(("arc", "trow"))),
        out_specs=(P(("arc", "trow"), "tcol"), P(None, "tcol", None)),
        check_vma=False,
    )
```

profile of v0, /device:TPU:19, one launch (start us, length us, event | category | flops | bytes accessed | tf_op | source)
XLA Modules:
  0.0 276.4 jit_solution(3097975123987560069)
XLA Ops:
  0.6 0.8 iota_compare_fusion.1
  1.5 1.4 slice_select_fusion.1
  2.9 0.7 collective-permute-start
  3.7 1.8 collective-permute-done
  5.5 1.8 dynamic-slice_select_fusion.2
  7.3 1.2 convolution_add_fusion.a_ref
  8.5 8.5 %local_inverse.1 = f32[2,128,128]{2,1,0:T(8,128)} custom-call(f32[2,128,128]{2,1,0:T(8,128)} %convolution_add_fusion.a_ref), custom_call_target="tpu_custom_call" | custom-call | tf_op jit(solution)/shard_map/local_inverse/pallas_call | solution.py:147
  17.0 1.4 convolution_convert_fusion.refs_0_.refs_5_
  18.6 0.4 collective-permute-start.1
  19.1 1.9 collective-permute-done.1
  20.9 1.2 broadcast_select_fusion.3.refs_2_
  22.2 2.2 broadcast_select_fusion.own_ref
  24.4 2.1 constant_dynamic-slice_fusion
  26.5 0.5 collective-permute-start.3
  27.0 1.2 collective-permute-start.11
  28.3 1.2 collective-permute-done.11
  29.5 1.3 collective-permute-start.2
  30.8 1.4 collective-permute-start.12
  32.4 1.0 collective-permute-done.12
  33.6 67.3 %collective-permute-done.16 = bf16[320,512]{1,0:T(8,128)(2,1)} collective-permute-done((bf16[320,512]{1,0:T(8,128)(2,1)}, bf16[320,512]{1,0:T(8,128)(2,1)}, u32[]{:S(2)}, u32[]{:S(2)}) %collective-permute-start.16) | collective-permute-done | bytes 327712 | tf_op jit(solution)/shard_map/ppermute | solution.py:103
  101.2 1.7 broadcast_select_fusion.4.refs_3_
  103.0 2.3 collective-permute-start.18
  105.3 3.2 %dynamic-slice_select_fusion = (bf16[320,1024]{1,0:T(8,128)(2,1)}, bf16[320,1024]{1,0:T(8,128)(2,1)}) fusion(bf16[640,1024]{1,0:T(8,128)(2,1)} %collective-permute-done.5, s32[]{:T(128)S(6)} %select_n.162, bf16[640,2048]{1,0:T(8,128)(2,1)S(1)} %broadcast_select_fusion.own_ref, s32[]{:T(128)S(6)} %select_n.176, s32[]{:T(128)S(6)} %select_n.185, pred[]{:T(512)S(6)} %eq.45, ...), kind=kLoop, calls=%fused_computation.3 | loop fusion | flops 655360 | bytes 3932178 | tf_op jit(solution)/shard_map/jit(_where)/select_n | solution.py:120
  108.5 1.2 collective-permute-start.4
  109.8 3.4 %collective-permute-done.13 = f32[4,1024]{1,0:T(4,128)S(1)} collective-permute-done((f32[4,1024]{1,0:T(4,128)S(1)}, f32[4,1024]{1,0:T(4,128)S(1)}, u32[]{:S(2)}, u32[]{:S(2)}) %collective-permute-start.13) | collective-permute-done | bytes 16416 | tf_op jit(solution)/shard_map/ppermute | solution.py:134
  113.3 1.2 collective-permute-start.10
  114.5 3.9 %collective-permute-done.10.refs_1_.refs_6_ = bf16[2,128,320]{2,1,0:T(8,128)(2,1)S(1)} collective-permute-done((bf16[2,128,320]{2,1,0:T(8,128)(2,1)S(1)}, bf16[2,128,320]{2,1,0:T(8,128)(2,1)S(1)}, u32[]{:S(2)}, u32[]{:S(2)}) %collective-permute-start.10) | collective-permute-done | bytes 163872 | tf_op jit(solution)/shard_map/ppermute | solution.py:103
  118.4 0.7 copy-done.4
  119.1 4.0 %collective-permute-start.7 = (bf16[320,1024]{1,0:T(8,128)(2,1)}, bf16[320,1024]{1,0:T(8,128)(2,1)}, u32[]{:S(2)}, u32[]{:S(2)}) collective-permute-start(bf16[320,1024]{1,0:T(8,128)(2,1)} %get-tuple-element.26), channel_id=1, source_target_pairs={{2,18},{3,19},{6,22},{7,23},{10,26},{11,27},{14,30},{15,31},{16,0}... | collective-permute-start | bytes 1966088 | tf_op jit(solution)/shard_map/ppermute | solution.py:103
  123.1 2.1 collective-permute-start.6
  125.2 1.3 collective-permute-start.21
  126.5 1.0 broadcast_select_fusion.5.refs_2_
  127.6 2.8 %collective-permute-start.17 = (bf16[320,512]{1,0:T(8,128)(2,1)S(1)}, bf16[320,512]{1,0:T(8,128)(2,1)S(1)}, u32[]{:S(2)}, u32[]{:S(2)}) collective-permute-start(bf16[320,512]{1,0:T(8,128)(2,1)S(1)} %broadcast_select_fusion.5.refs_2_), channel_id=1, source_target_pairs={{0,1},{1,0},{2,3},{3,2},{4,5},{5,4},{6,7},{7,6},{8,9},{9,8},{10,11... | collective-permute-start | bytes 983048 | tf_op jit(solution)/shard_map/ppermute | solution.py:112
  130.4 2.0 broadcast_select_fusion.2.refs_1_
  132.4 16.0 %collective-permute-done.7 = bf16[320,1024]{1,0:T(8,128)(2,1)} collective-permute-done((bf16[320,1024]{1,0:T(8,128)(2,1)}, bf16[320,1024]{1,0:T(8,128)(2,1)}, u32[]{:S(2)}, u32[]{:S(2)}) %collective-permute-start.7) | collective-permute-done | bytes 655392 | tf_op jit(solution)/shard_map/ppermute | solution.py:103
  148.4 1.5 collective-permute-start.20
  149.9 1.5 collective-permute-start.19
  151.4 2.0 broadcast_select_fusion.1.refs_2_
  153.4 3.1 %collective-permute-start.9 = (bf16[320,1024]{1,0:T(8,128)(2,1)}, bf16[320,1024]{1,0:T(8,128)(2,1)}, u32[]{:S(2)}, u32[]{:S(2)}) collective-permute-start(bf16[320,1024]{1,0:T(8,128)(2,1)} %broadcast_select_fusion.1.refs_2_), channel_id=1, source_target_pairs={{0,1},{1,0},{2,3},{3,2},{4,5},{5,4},{6,7},{7,6},{8,9},{9,8},{10,11... | collective-permute-start | bytes 1966088 | tf_op jit(solution)/shard_map/ppermute | solution.py:112
  156.6 0.9 copy-done.6
  157.4 1.1 collective-permute-start.8
  158.5 0.7 stack.86.table_ref
  159.2 0.6 stack.84.table_ref
  159.8 0.6 stack.83.table_ref
  160.5 0.6 fusion.5
  161.1 26.8 %shard_map.59 = (bf16[1280,512]{1,0:T(8,128)(2,1)}, f32[512,512]{1,0:T(8,128)}, bf16[1280,512]{1,0:T(8,128)(2,1)}, bf16[1280,512]{1,0:T(8,128)(2,1)}, f32[512,512]{1,0:T(8,128)}) custom-call(s32[12]{0:T(128)} %stack.84.table_ref, f32[1,512]{1,0:T(1,128)} %bitcast.33, bf16[2,128,320]{2,1,0:T(8,128)(2,1)} %copy-done.2, bf16[2,128,320]{2,1,0:T(8,128)(2,1)} %copy-done.4, ...), custom_call_target="tpu_custom_call" | custom-call | tf_op jit(solution)/shard_map/pallas_call | solution.py:339
  187.9 33.8 %shard_map.60 = (bf16[1280,512]{1,0:T(8,128)(2,1)}, bf16[1280,512]{1,0:T(8,128)(2,1)}, f32[512,512]{1,0:T(8,128)}) custom-call(s32[12]{0:T(128)} %stack.86.table_ref, f32[1,512]{1,0:T(1,128)} %bitcast.32, bf16[2,128,320]{2,1,0:T(8,128)(2,1)} %copy-done.2, bf16[2,128,320]{2,1,0:T(8,128)(2,1)} %copy-done.4, bf16[640,512]{1,0:T(8,128)(2,1)} %copy-done.3, ...), custom_call_target="tpu_custom_call" | custom-call | tf_op jit(solution)/shard_map/pallas_call | solution.py:339
  221.8 54.7 %assemble.1 = (f32[1024,2048]{1,0:T(8,128)}, f32[2,2048,512]{2,1,0:T(8,128)}) custom-call(s32[26]{0:T(128)} %stack.83.table_ref, bf16[640,2048]{1,0:T(8,128)(2,1)} %copy-done, bf16[640,2048]{1,0:T(8,128)(2,1)} %collective-permute-done.2.refs_0_, bf16[320,1024]{1,0:T(8,128)(2,1)} %broadcast_select_fusion.2.refs_1_, ...), custom_call_target="tpu_custom_call" | custom-call | tf_op jit(solution)/shard_map/assemble/pallas_call | solution.py:444
  (53 shorter events, 1.4 us)
Async XLA Ops:
  0.6 6.7 %copy-start.8 = (bf16[640,128]{1,0:T(8,128)(2,1)S(1)}, bf16[640,128]{1,0:T(8,128)(2,1)}, u32[]{:S(2)}) copy-start(bf16[640,128]{1,0:T(8,128)(2,1)} %param.5) | copy-start | bytes 491524
  1.5 16.9 %copy-start.1 = (bf16[640,2048]{1,0:T(8,128)(2,1)S(1)}, bf16[640,2048]{1,0:T(8,128)(2,1)}, u32[]{:S(2)}) copy-start(bf16[640,2048]{1,0:T(8,128)(2,1)} %param.4) | copy-start | bytes 7864324
  2.9 2.6 collective-permute-start
  18.4 94.9 %copy-start.2 = (bf16[2,128,320]{2,1,0:T(8,128)(2,1)}, bf16[2,128,320]{2,1,0:T(8,128)(2,1)S(1)}, u32[]{:S(2)}) copy-start(bf16[2,128,320]{2,1,0:T(8,128)(2,1)S(1)} %convolution_convert_fusion.refs_0_.refs_5_) | copy-start | bytes 491524
  18.6 2.3 collective-permute-start.1
  22.2 127.8 %copy-start.3 = (bf16[640,512]{1,0:T(8,128)(2,1)}, bf16[640,512]{1,0:T(8,128)(2,1)S(1)}, u32[]{:S(2)}) copy-start(bf16[640,512]{1,0:T(8,128)(2,1)S(1)} %broadcast_select_fusion.3.refs_2_) | copy-start | bytes 1966084
  24.4 80.9 %copy-start = (bf16[640,2048]{1,0:T(8,128)(2,1)}, bf16[640,2048]{1,0:T(8,128)(2,1)S(1)}, u32[]{:S(2)}) copy-start(bf16[640,2048]{1,0:T(8,128)(2,1)S(1)} %broadcast_select_fusion.own_ref) | copy-start | bytes 7864324
  24.4 2.6 copy-start.9
  26.5 78.8 %collective-permute-start.5 = (bf16[640,1024]{1,0:T(8,128)(2,1)}, bf16[640,1024]{1,0:T(8,128)(2,1)}, u32[]{:S(2)}, u32[]{:S(2)}) collective-permute-start(bf16[640,1024]{1,0:T(8,128)(2,1)} %get-tuple-element.28), channel_id=1, source_target_pairs={{0,1},{1,0},{2,3},{3,2},{4,5},{5,4},{6,7},{7,6},{8,9},{9,8},{10,11... | collective-permute-start | bytes 3932168 | tf_op jit(solution)/shard_map/ppermute | solution.py:112
  26.5 78.8 %collective-permute-start.3 = (bf16[640,1024]{1,0:T(8,128)(2,1)}, bf16[640,1024]{1,0:T(8,128)(2,1)}, u32[]{:S(2)}, u32[]{:S(2)}) collective-permute-start(bf16[640,1024]{1,0:T(8,128)(2,1)} %get-tuple-element.29), channel_id=1, source_target_pairs={{0,1},{1,0},{2,3},{3,2},{4,5},{5,4},{6,7},{7,6},{8,9},{9,8},{10,11... | collective-permute-start | bytes 3932168 | tf_op jit(solution)/shard_map/ppermute | solution.py:112
  27.0 2.5 collective-permute-start.11
  29.5 192.3 %collective-permute-start.2 = (bf16[640,2048]{1,0:T(8,128)(2,1)S(1)}, bf16[640,2048]{1,0:T(8,128)(2,1)}, u32[]{:S(2)}, u32[]{:S(2)}) collective-permute-start(bf16[640,2048]{1,0:T(8,128)(2,1)S(1)} %broadcast_select_fusion.own_ref), channel_id=1, source_target_pairs={{0,16},{1,17},{2,18},{3,19},{4,20},{5,21},{6,22},{7,23},{8,24},{9,... | collective-permute-start | bytes 7864328 | tf_op jit(solution)/shard_map/ppermute | solution.py:103
  30.8 2.6 collective-permute-start.12
  32.2 68.8 %collective-permute-start.16 = (bf16[320,512]{1,0:T(8,128)(2,1)}, bf16[320,512]{1,0:T(8,128)(2,1)}, u32[]{:S(2)}, u32[]{:S(2)}) collective-permute-start(bf16[320,512]{1,0:T(8,128)(2,1)} %dynamic-slice_select_fusion.2), channel_id=1, source_target_pairs={{0,16},{1,17},{2,18},{3,19},{4,20},{5,21},{6,22},{7,23},{8,24},{9,... | collective-permute-start | bytes 983048 | tf_op jit(solution)/shard_map/ppermute | solution.py:103
  33.4 67.9 %collective-permute-start.15 = (bf16[320,512]{1,0:T(8,128)(2,1)}, bf16[320,512]{1,0:T(8,128)(2,1)}, u32[]{:S(2)}, u32[]{:S(2)}) collective-permute-start(bf16[320,512]{1,0:T(8,128)(2,1)} %dynamic-slice_select_fusion.2), channel_id=1, source_target_pairs={{0,18},{1,19},{2,16},{3,17},{4,22},{5,23},{6,20},{7,21},{8,26},{9,... | collective-permute-start | bytes 983048 | tf_op jit(solution)/shard_map/ppermute | solution.py:103
  101.0 22.1 %collective-permute-start.14 = (bf16[320,512]{1,0:T(8,128)(2,1)}, bf16[320,512]{1,0:T(8,128)(2,1)}, u32[]{:S(2)}, u32[]{:S(2)}) collective-permute-start(bf16[320,512]{1,0:T(8,128)(2,1)} %dynamic-slice_select_fusion.2), channel_id=1, source_target_pairs={{0,2},{1,3},{2,0},{3,1},{4,6},{5,7},{6,4},{7,5},{8,10},{9,11},{10,... | collective-permute-start | bytes 983048 | tf_op jit(solution)/shard_map/ppermute | solution.py:103
  103.0 22.2 %collective-permute-start.18 = (bf16[320,512]{1,0:T(8,128)(2,1)}, bf16[320,512]{1,0:T(8,128)(2,1)}, u32[]{:S(2)}, u32[]{:S(2)}) collective-permute-start(bf16[320,512]{1,0:T(8,128)(2,1)} %broadcast_select_fusion.4.refs_3_), channel_id=1, source_target_pairs={{0,1},{1,0},{2,3},{3,2},{4,5},{5,4},{6,7},{7,6},{8,9},{9,8},{10,11... | collective-permute-start | bytes 983048 | tf_op jit(solution)/shard_map/ppermute | solution.py:112
  108.5 19.1 %collective-permute-start.4 = (bf16[320,1024]{1,0:T(8,128)(2,1)}, bf16[320,1024]{1,0:T(8,128)(2,1)}, u32[]{:S(2)}, u32[]{:S(2)}) collective-permute-start(bf16[320,1024]{1,0:T(8,128)(2,1)} %get-tuple-element.27), channel_id=1, source_target_pairs={{0,2},{1,3},{2,0},{3,1},{4,6},{5,7},{6,4},{7,5},{8,10},{9,11},{10,... | collective-permute-start | bytes 1966088 | tf_op jit(solution)/shard_map/ppermute | solution.py:103
  109.7 3.6 %collective-permute-start.13 = (f32[4,1024]{1,0:T(4,128)S(1)}, f32[4,1024]{1,0:T(4,128)S(1)}, u32[]{:S(2)}, u32[]{:S(2)}) collective-permute-start(f32[4,1024]{1,0:T(4,128)S(1)} %pad_maximum_fusion.1), channel_id=1, source_target_pairs={{0,8},{1,9},{2,10},{3,11},{4,12},{5,13},{6,14},{7,15},{8,0},{9,1},... | collective-permute-start | bytes 49160 | tf_op jit(solution)/shard_map/ppermute | solution.py:134
  113.3 5.1 %collective-permute-start.10 = (bf16[2,128,320]{2,1,0:T(8,128)(2,1)S(1)}, bf16[2,128,320]{2,1,0:T(8,128)(2,1)S(1)}, u32[]{:S(2)}, u32[]{:S(2)}) collective-permute-start(bf16[2,128,320]{2,1,0:T(8,128)(2,1)S(1)} %convolution_convert_fusion.refs_0_.refs_5_), channel_id=1, source_target_pairs={{0,16},{1,17},{2,18},{3,19},{4,20},{5,21},{6,22},{7,23},{8,24},{9,... | collective-permute-start | bytes 491528 | tf_op jit(solution)/shard_map/ppermute | solution.py:103
  118.4 0.7 copy-start.4
  119.1 29.4 %collective-permute-start.7 = (bf16[320,1024]{1,0:T(8,128)(2,1)}, bf16[320,1024]{1,0:T(8,128)(2,1)}, u32[]{:S(2)}, u32[]{:S(2)}) collective-permute-start(bf16[320,1024]{1,0:T(8,128)(2,1)} %get-tuple-element.26), channel_id=1, source_target_pairs={{2,18},{3,19},{6,22},{7,23},{10,26},{11,27},{14,30},{15,31},{16,0}... | collective-permute-start | bytes 1966088 | tf_op jit(solution)/shard_map/ppermute | solution.py:103
  123.1 26.9 %collective-permute-start.6 = (bf16[320,1024]{1,0:T(8,128)(2,1)}, bf16[320,1024]{1,0:T(8,128)(2,1)}, u32[]{:S(2)}, u32[]{:S(2)}) collective-permute-start(bf16[320,1024]{1,0:T(8,128)(2,1)} %get-tuple-element.26), channel_id=1, source_target_pairs={{2,16},{3,17},{6,20},{7,21},{10,24},{11,25},{14,28},{15,29},{16,2}... | collective-permute-start | bytes 1966088 | tf_op jit(solution)/shard_map/ppermute | solution.py:103
  125.2 31.3 %collective-permute-start.21 = (bf16[640,512]{1,0:T(8,128)(2,1)S(1)}, bf16[640,512]{1,0:T(8,128)(2,1)S(1)}, u32[]{:S(2)}, u32[]{:S(2)}) collective-permute-start(bf16[640,512]{1,0:T(8,128)(2,1)S(1)} %broadcast_select_fusion.3.refs_2_), channel_id=1, source_target_pairs={{0,18},{1,19},{4,22},{5,23},{8,26},{9,27},{12,30},{13,31},{16,2},{... | collective-permute-start | bytes 1966088 | tf_op jit(solution)/shard_map/ppermute | solution.py:103
  127.6 25.9 %copy-start.5 = (bf16[320,512]{1,0:T(8,128)(2,1)}, bf16[320,512]{1,0:T(8,128)(2,1)S(1)}, u32[]{:S(2)}) copy-start(bf16[320,512]{1,0:T(8,128)(2,1)S(1)} %broadcast_select_fusion.5.refs_2_) | copy-start | bytes 983044
  127.6 25.9 %collective-permute-start.17 = (bf16[320,512]{1,0:T(8,128)(2,1)S(1)}, bf16[320,512]{1,0:T(8,128)(2,1)S(1)}, u32[]{:S(2)}, u32[]{:S(2)}) collective-permute-start(bf16[320,512]{1,0:T(8,128)(2,1)S(1)} %broadcast_select_fusion.5.refs_2_), channel_id=1, source_target_pairs={{0,1},{1,0},{2,3},{3,2},{4,5},{5,4},{6,7},{7,6},{8,9},{9,8},{10,11... | collective-permute-start | bytes 983048 | tf_op jit(solution)/shard_map/ppermute | solution.py:112
  148.4 39.5 %collective-permute-start.20 = (bf16[640,512]{1,0:T(8,128)(2,1)S(1)}, bf16[640,512]{1,0:T(8,128)(2,1)}, u32[]{:S(2)}, u32[]{:S(2)}) collective-permute-start(bf16[640,512]{1,0:T(8,128)(2,1)S(1)} %broadcast_select_fusion.3.refs_2_), channel_id=1, source_target_pairs={{0,16},{1,17},{4,20},{5,21},{8,24},{9,25},{12,28},{13,29},{16,0},{... | collective-permute-start | bytes 1966088 | tf_op jit(solution)/shard_map/ppermute | solution.py:103
  149.9 38.0 %collective-permute-start.19 = (bf16[640,512]{1,0:T(8,128)(2,1)S(1)}, bf16[640,512]{1,0:T(8,128)(2,1)}, u32[]{:S(2)}, u32[]{:S(2)}) collective-permute-start(bf16[640,512]{1,0:T(8,128)(2,1)S(1)} %broadcast_select_fusion.3.refs_2_), channel_id=1, source_target_pairs={{0,2},{1,3},{4,6},{5,7},{8,10},{9,11},{12,14},{13,15},{16,18},{17,... | collective-permute-start | bytes 1966088 | tf_op jit(solution)/shard_map/ppermute | solution.py:103
  153.4 3.1 %copy-start.7 = (bf16[320,512]{1,0:T(8,128)(2,1)}, bf16[320,512]{1,0:T(8,128)(2,1)S(1)}, u32[]{:S(2)}) copy-start(bf16[320,512]{1,0:T(8,128)(2,1)S(1)} %collective-permute-done.17.refs_4_) | copy-start | bytes 983044
  153.4 68.3 %collective-permute-start.9 = (bf16[320,1024]{1,0:T(8,128)(2,1)}, bf16[320,1024]{1,0:T(8,128)(2,1)}, u32[]{:S(2)}, u32[]{:S(2)}) collective-permute-start(bf16[320,1024]{1,0:T(8,128)(2,1)} %broadcast_select_fusion.1.refs_2_), channel_id=1, source_target_pairs={{0,1},{1,0},{2,3},{3,2},{4,5},{5,4},{6,7},{7,6},{8,9},{9,8},{10,11... | collective-permute-start | bytes 1966088 | tf_op jit(solution)/shard_map/ppermute | solution.py:112
  156.6 0.9 copy-start.6
  157.4 64.3 %collective-permute-start.8 = (bf16[320,1024]{1,0:T(8,128)(2,1)}, bf16[320,1024]{1,0:T(8,128)(2,1)}, u32[]{:S(2)}, u32[]{:S(2)}) collective-permute-start(bf16[320,1024]{1,0:T(8,128)(2,1)} %broadcast_select_fusion.2.refs_1_), channel_id=1, source_target_pairs={{0,1},{1,0},{2,3},{3,2},{4,5},{5,4},{6,7},{7,6},{8,9},{9,8},{10,11... | collective-permute-start | bytes 1966088 | tf_op jit(solution)/shard_map/ppermute | solution.py:112
where the time goes:
time: 281 us; the launch traced here: 276 us
  Pallas kernels  124 us (44%)
  waiting for transfers between devices  96.5 us (34%)
  starting transfers between devices  28.5 us (10%)
  other arithmetic  17.7 us (6%)
  local copies, waits for them, and re-layouts  6.39 us (2%)
    ppermute x11, waiting for transfers between devices, move(): return lax.ppermute(block, AXES, pairs)  87.3 us
    pallas_call x2, Pallas kernels, pivot_call(): pl.pallas_call(functools.partial(kernel, len(basis), len(pieces), layout)...  60.6 us
    pallas_call x1, Pallas kernels, assemble(): pl.pallas_call(functools.partial(assemble_kernel, (arcs, own_arcs, len(ti...  54.7 us
    ppermute x11, starting transfers between devices, move(): return lax.ppermute(block, AXES, pairs)  14.8 us
    ppermute x8, starting transfers between devices, core_swap(): return lax.ppermute(block, AXES, pairs)  11 us
    pallas_call x1, Pallas kernels, local_call(): pl.pallas_call(local_kernel, out_shape=jax.ShapeDtypeStruct(a.shape, jnp....  8.51 us
    ppermute x3, waiting for transfers between devices, gather_rows(): got = lax.ppermute(tile, AXES, pairs)  5.63 us
  transfers between devices with their start and end apart: 22, of which 8 were waited for; matrix products, arithmetic and copies ran while one was open for 5% of the time, Pallas kernels for 22%

commit v1 on v0

--- a/solution.py
+++ b/solution.py
@@ -46,6 +46,8 @@
             for k in range(SUB)
         }
         rest = {t: jnp.where(inside, 0.0, rows[t]) for t in below}
+        soon = below[:1]
+        factor, inverses = {}, {}
         for k in range(0, SUB, 2):
             a, b, c = sp[k, k], sp[k + 1, k], sp[k + 1, k + 1]
             det = a * c - b * b
@@ -63,15 +65,25 @@
                 for n in range(m, SUB):
                     sp[n, m] = sp[n, m] - (sp[n, k] * pair[m][0] + sp[n, k + 1] * pair[m][1]) * scale
             for at, inv, l in ((k, first, one), (k + 1, second, two)):
+                factor[at], inverses[at] = l, inv
                 z[at] = z[at] * inv
                 for m in range(at + 1, SUB):
                     z[m] = z[m] - l[m] * z[at]
-                for t in below:
+                for t in soon:
                     coef = col[t, at] * inv
                     for m in range(at + 1, SUB):
                         col[t, m] = col[t, m] - coef * l[m]
                     rest[t] = rest[t] - coef * z[at]
+        back = {}
+        for k in reversed(range(SUB)):
+            back[k] = z[k]
+            for m in range(k + 1, SUB):
+                back[k] = back[k] - factor[k][m] * back[m]
+            back[k] = back[k] * inverses[k]
         for t in below:
+            if t not in soon:
+                for k in range(SUB):
+                    rest[t] = rest[t] - col[t, k] * back[k]
             rows[t] = rest[t]
         done = z[0]
         for k in range(1, SUB):
@@ -259,7 +271,7 @@
 
 def weigh(terms, top_ref, rest_ref):
     rows = top_ref.shape[0]
-    chunk = next(n for n in (512, 320, 256, LANES, SUB) if rows % n == 0 and rows > n)
+    chunk = next(n for n in (640, 512, 320, 256, LANES, SUB) if rows % n == 0 and rows > n)
     parts = [(ref, *split(factor)) for ref, factor in terms]
 
     def step(i, carry):
@@ -411,19 +423,21 @@
     lax.fori_loop(0, width // chunk, col_chunk, 0)
     d = d_ref[:, pl.ds(pl.multiple_of(jnp.clip(tile_start - row_start, 0, tile_rows - width), LANES), width)]
 
+    tall = min(2 * CHUNK, tile_rows)
+
     def normal_chunk(i, carry):
-        at = pl.ds(pl.multiple_of(i * chunk, chunk), chunk)
+        at = pl.ds(pl.multiple_of(i * tall, tall), tall)
         dims = ((1,), (1,))
         value = product(xrt[at, :], xc[...], ((1,), (0,))) - (
             product(fr_top[at, :], fc_top[...], dims)
             + (product(fr_top[at, :], fc_rest[...], dims) + product(fr_rest[at, :], fc_top[...], dims))
         )
-        row = lax.broadcasted_iota(jnp.int32, (chunk, width), 0) + (row_start + i * chunk)
-        col = lax.broadcasted_iota(jnp.int32, (chunk, width), 1) + tile_start
+        row = lax.broadcasted_iota(jnp.int32, (tall, width), 0) + (row_start + i * tall)
+        col = lax.broadcasted_iota(jnp.int32, (tall, width), 1) + tile_start
         normal_ref[at, :] = value + jnp.where(row == col, d, 0.0)
         return carry
 
-    lax.fori_loop(0, tile_rows // chunk, normal_chunk, 0)
+    lax.fori_loop(0, tile_rows // tall, normal_chunk, 0)
 
 
 def assemble(own, got, tiles, layout, basis, tops, rests, mds, regularizer, table, own_arcs):
@@ -510,7 +524,7 @@
     def spread_lead(mine, source):
         return [
             [
-                plan.move(mine, s, dx, source) if s or dx else mine
+                plan.move(mine, s, dx, source if s else None) if s or dx else mine
                 for dx in range(plan.across)
             ]
             for s in range(plan.arc)

time: 281 us -> 275 us (0.979); the launches traced: 276 us -> 274 us
  Pallas kernels: 124 us -> 120 us
    ppermute x8, starting transfers between devices: 11 us -> 14.3 us  [core_swap(): return lax.ppermute(block, AXES, pairs)]
  transfers between devices with their start and end apart: 22 -> 22, of which waited for: 8 -> 8; matrix products, arithmetic and copies ran while one was open for 5% -> 5% of each run, Pallas kernels for 22% -> 21%
where the time goes in v1:
time: 275 us; the launch traced here: 274 us
  Pallas kernels  120 us (44%)
  waiting for transfers between devices  96.5 us (35%)
  starting transfers between devices  30.4 us (11%)
  other arithmetic  17.7 us (6%)
  local copies, waits for them, and re-layouts  6.39 us (2%)
    ppermute x11, waiting for transfers between devices, move(): return lax.ppermute(block, AXES, pairs)  87.3 us
    pallas_call x2, Pallas kernels, pivot_call(): pl.pallas_call(functools.partial(kernel, len(basis), len(pieces), layout)...  58.5 us
    pallas_call x1, Pallas kernels, assemble(): pl.pallas_call(functools.partial(assemble_kernel, (arcs, own_arcs, len(ti...  52.8 us
    ppermute x8, starting transfers between devices, core_swap(): return lax.ppermute(block, AXES, pairs)  14.3 us
    ppermute x11, starting transfers between devices, move(): return lax.ppermute(block, AXES, pairs)  13.4 us
    pallas_call x1, Pallas kernels, local_call(): pl.pallas_call(local_kernel, out_shape=jax.ShapeDtypeStruct(a.shape, jnp....  8.61 us
    ppermute x3, waiting for transfers between devices, gather_rows(): got = lax.ppermute(tile, AXES, pairs)  5.63 us
  transfers between devices with their start and end apart: 22, of which 8 were waited for; matrix products, arithmetic and copies ran while one was open for 5% of the time, Pallas kernels for 21%

profile of v1, /device:TPU:19, one launch (start us, length us, event | category | flops | bytes accessed | tf_op | source)
XLA Modules:
  0.0 274.4 jit_solution(511818196283589574)
XLA Ops:
  0.6 0.8 iota_compare_fusion.1
  1.5 1.4 slice_select_fusion.1
  2.9 0.7 collective-permute-start
  3.7 1.8 collective-permute-done
  5.5 1.8 dynamic-slice_select_fusion.2
  7.3 1.2 convolution_add_fusion.a_ref
  8.5 8.6 %local_inverse.1 = f32[2,128,128]{2,1,0:T(8,128)} custom-call(f32[2,128,128]{2,1,0:T(8,128)} %convolution_add_fusion.a_ref), custom_call_target="tpu_custom_call" | custom-call | tf_op jit(solution)/shard_map/local_inverse/pallas_call | solution.py:159
  17.1 1.4 convolution_convert_fusion.refs_0_.refs_5_
  18.7 0.4 collective-permute-start.1
  19.1 1.9 collective-permute-done.1
  21.0 1.2 broadcast_select_fusion.3.refs_2_
  22.3 2.2 broadcast_select_fusion.own_ref
  24.5 2.1 constant_dynamic-slice_fusion
  26.6 0.5 collective-permute-start.3
  27.1 1.2 collective-permute-start.11
  28.4 1.2 collective-permute-done.11
  29.6 1.3 collective-permute-start.2
  30.9 1.4 collective-permute-start.12
  32.5 1.0 collective-permute-done.12
  33.7 67.3 %collective-permute-done.16 = bf16[320,512]{1,0:T(8,128)(2,1)} collective-permute-done((bf16[320,512]{1,0:T(8,128)(2,1)}, bf16[320,512]{1,0:T(8,128)(2,1)}, u32[]{:S(2)}, u32[]{:S(2)}) %collective-permute-start.16) | collective-permute-done | bytes 327712 | tf_op jit(solution)/shard_map/ppermute | solution.py:115
  101.1 0.3 collective-permute-start.14
  101.3 1.7 broadcast_select_fusion.4.refs_3_
  103.1 2.3 collective-permute-start.18
  105.4 3.2 %dynamic-slice_select_fusion = (bf16[320,1024]{1,0:T(8,128)(2,1)}, bf16[320,1024]{1,0:T(8,128)(2,1)}) fusion(bf16[640,1024]{1,0:T(8,128)(2,1)} %collective-permute-done.5, s32[]{:T(128)S(6)} %select_n.162, bf16[640,2048]{1,0:T(8,128)(2,1)S(1)} %broadcast_select_fusion.own_ref, s32[]{:T(128)S(6)} %select_n.176, s32[]{:T(128)S(6)} %select_n.185, pred[]{:T(512)S(6)} %eq.45, ...), kind=kLoop, calls=%fused_computation.3 | loop fusion | flops 655360 | bytes 3932178 | tf_op jit(solution)/shard_map/jit(_where)/select_n | solution.py:132
  108.6 1.2 collective-permute-start.4
  109.9 3.4 %collective-permute-done.13 = f32[4,1024]{1,0:T(4,128)S(1)} collective-permute-done((f32[4,1024]{1,0:T(4,128)S(1)}, f32[4,1024]{1,0:T(4,128)S(1)}, u32[]{:S(2)}, u32[]{:S(2)}) %collective-permute-start.13) | collective-permute-done | bytes 16416 | tf_op jit(solution)/shard_map/ppermute | solution.py:146
  113.4 1.2 collective-permute-start.10
  114.6 3.9 %collective-permute-done.10.refs_1_.refs_6_ = bf16[2,128,320]{2,1,0:T(8,128)(2,1)S(1)} collective-permute-done((bf16[2,128,320]{2,1,0:T(8,128)(2,1)S(1)}, bf16[2,128,320]{2,1,0:T(8,128)(2,1)S(1)}, u32[]{:S(2)}, u32[]{:S(2)}) %collective-permute-start.10) | collective-permute-done | bytes 163872 | tf_op jit(solution)/shard_map/ppermute | solution.py:115
  118.5 0.7 copy-done.4
  119.2 4.0 %collective-permute-start.7 = (bf16[320,1024]{1,0:T(8,128)(2,1)}, bf16[320,1024]{1,0:T(8,128)(2,1)}, u32[]{:S(2)}, u32[]{:S(2)}) collective-permute-start(bf16[320,1024]{1,0:T(8,128)(2,1)} %get-tuple-element.26), channel_id=1, source_target_pairs={{2,18},{3,19},{6,22},{7,23},{10,26},{11,27},{14,30},{15,31},{16,0}... | collective-permute-start | bytes 1966088 | tf_op jit(solution)/shard_map/ppermute | solution.py:115
  123.2 2.1 collective-permute-start.6
  125.3 1.3 collective-permute-start.21
  126.6 1.0 broadcast_select_fusion.5.refs_2_
  127.7 2.8 %collective-permute-start.17 = (bf16[320,512]{1,0:T(8,128)(2,1)S(1)}, bf16[320,512]{1,0:T(8,128)(2,1)S(1)}, u32[]{:S(2)}, u32[]{:S(2)}) collective-permute-start(bf16[320,512]{1,0:T(8,128)(2,1)S(1)} %broadcast_select_fusion.5.refs_2_), channel_id=1, source_target_pairs={{0,1},{1,0},{2,3},{3,2},{4,5},{5,4},{6,7},{7,6},{8,9},{9,8},{10,11... | collective-permute-start | bytes 983048 | tf_op jit(solution)/shard_map/ppermute | solution.py:124
  130.5 2.0 broadcast_select_fusion.2.refs_1_
  132.5 16.0 %collective-permute-done.7 = bf16[320,1024]{1,0:T(8,128)(2,1)} collective-permute-done((bf16[320,1024]{1,0:T(8,128)(2,1)}, bf16[320,1024]{1,0:T(8,128)(2,1)}, u32[]{:S(2)}, u32[]{:S(2)}) %collective-permute-start.7) | collective-permute-done | bytes 655392 | tf_op jit(solution)/shard_map/ppermute | solution.py:115
  148.5 1.5 collective-permute-start.20
  150.0 2.0 broadcast_select_fusion.1.refs_2_
  152.1 3.1 %collective-permute-start.9 = (bf16[320,1024]{1,0:T(8,128)(2,1)}, bf16[320,1024]{1,0:T(8,128)(2,1)}, u32[]{:S(2)}, u32[]{:S(2)}) collective-permute-start(bf16[320,1024]{1,0:T(8,128)(2,1)} %broadcast_select_fusion.1.refs_2_), channel_id=1, source_target_pairs={{0,1},{1,0},{2,3},{3,2},{4,5},{5,4},{6,7},{7,6},{8,9},{9,8},{10,11... | collective-permute-start | bytes 1966088 | tf_op jit(solution)/shard_map/ppermute | solution.py:124
  155.2 0.9 copy-done.6
  156.0 4.4 %collective-permute-start.8 = (bf16[320,1024]{1,0:T(8,128)(2,1)}, bf16[320,1024]{1,0:T(8,128)(2,1)}, u32[]{:S(2)}, u32[]{:S(2)}) collective-permute-start(bf16[320,1024]{1,0:T(8,128)(2,1)} %broadcast_select_fusion.2.refs_1_), channel_id=1, source_target_pairs={{0,1},{1,0},{2,3},{3,2},{4,5},{5,4},{6,7},{7,6},{8,9},{9,8},{10,11... | collective-permute-start | bytes 1966088 | tf_op jit(solution)/shard_map/ppermute | solution.py:124
  160.5 0.7 stack.86.table_ref
  161.2 0.6 stack.84.table_ref
  161.8 0.6 stack.83.table_ref
  162.5 0.6 fusion.5
  163.1 25.6 %shard_map.59 = (bf16[1280,512]{1,0:T(8,128)(2,1)}, f32[512,512]{1,0:T(8,128)}, bf16[1280,512]{1,0:T(8,128)(2,1)}, bf16[1280,512]{1,0:T(8,128)(2,1)}, f32[512,512]{1,0:T(8,128)}) custom-call(s32[12]{0:T(128)} %stack.84.table_ref, f32[1,512]{1,0:T(1,128)} %bitcast.33, bf16[2,128,320]{2,1,0:T(8,128)(2,1)} %copy-done.2, bf16[2,128,320]{2,1,0:T(8,128)(2,1)} %copy-done.4, ...), custom_call_target="tpu_custom_call" | custom-call | tf_op jit(solution)/shard_map/pallas_call | solution.py:351
  188.7 32.9 %shard_map.60 = (bf16[1280,512]{1,0:T(8,128)(2,1)}, bf16[1280,512]{1,0:T(8,128)(2,1)}, f32[512,512]{1,0:T(8,128)}) custom-call(s32[12]{0:T(128)} %stack.86.table_ref, f32[1,512]{1,0:T(1,128)} %bitcast.32, bf16[2,128,320]{2,1,0:T(8,128)(2,1)} %copy-done.2, bf16[2,128,320]{2,1,0:T(8,128)(2,1)} %copy-done.4, bf16[640,512]{1,0:T(8,128)(2,1)} %copy-done.3, ...), custom_call_target="tpu_custom_call" | custom-call | tf_op jit(solution)/shard_map/pallas_call | solution.py:351
  221.6 52.8 %assemble.1 = (f32[1024,2048]{1,0:T(8,128)}, f32[2,2048,512]{2,1,0:T(8,128)}) custom-call(s32[26]{0:T(128)} %stack.83.table_ref, bf16[640,2048]{1,0:T(8,128)(2,1)} %copy-done, bf16[640,2048]{1,0:T(8,128)(2,1)} %collective-permute-done.2.refs_0_, bf16[320,1024]{1,0:T(8,128)(2,1)} %broadcast_select_fusion.2.refs_1_, ...), custom_call_target="tpu_custom_call" | custom-call | tf_op jit(solution)/shard_map/assemble/pallas_call | solution.py:458
  (53 shorter events, 1.2 us)
Async XLA Ops:
  0.6 6.7 %copy-start.8 = (bf16[640,128]{1,0:T(8,128)(2,1)S(1)}, bf16[640,128]{1,0:T(8,128)(2,1)}, u32[]{:S(2)}) copy-start(bf16[640,128]{1,0:T(8,128)(2,1)} %param.5) | copy-start | bytes 491524
  1.5 17.0 %copy-start.1 = (bf16[640,2048]{1,0:T(8,128)(2,1)S(1)}, bf16[640,2048]{1,0:T(8,128)(2,1)}, u32[]{:S(2)}) copy-start(bf16[640,2048]{1,0:T(8,128)(2,1)} %param.4) | copy-start | bytes 7864324
  2.9 2.6 collective-permute-start
  18.5 94.9 %copy-start.2 = (bf16[2,128,320]{2,1,0:T(8,128)(2,1)}, bf16[2,128,320]{2,1,0:T(8,128)(2,1)S(1)}, u32[]{:S(2)}) copy-start(bf16[2,128,320]{2,1,0:T(8,128)(2,1)S(1)} %convolution_convert_fusion.refs_0_.refs_5_) | copy-start | bytes 491524
  18.7 2.3 collective-permute-start.1
  22.2 127.8 %copy-start.3 = (bf16[640,512]{1,0:T(8,128)(2,1)}, bf16[640,512]{1,0:T(8,128)(2,1)S(1)}, u32[]{:S(2)}) copy-start(bf16[640,512]{1,0:T(8,128)(2,1)S(1)} %broadcast_select_fusion.3.refs_2_) | copy-start | bytes 1966084
  24.5 80.9 %copy-start = (bf16[640,2048]{1,0:T(8,128)(2,1)}, bf16[640,2048]{1,0:T(8,128)(2,1)S(1)}, u32[]{:S(2)}) copy-start(bf16[640,2048]{1,0:T(8,128)(2,1)S(1)} %broadcast_select_fusion.own_ref) | copy-start | bytes 7864324
  24.5 2.6 copy-start.9
  26.6 78.8 %collective-permute-start.5 = (bf16[640,1024]{1,0:T(8,128)(2,1)}, bf16[640,1024]{1,0:T(8,128)(2,1)}, u32[]{:S(2)}, u32[]{:S(2)}) collective-permute-start(bf16[640,1024]{1,0:T(8,128)(2,1)} %get-tuple-element.28), channel_id=1, source_target_pairs={{0,1},{1,0},{2,3},{3,2},{4,5},{5,4},{6,7},{7,6},{8,9},{9,8},{10,11... | collective-permute-start | bytes 3932168 | tf_op jit(solution)/shard_map/ppermute | solution.py:124
  26.6 78.8 %collective-permute-start.3 = (bf16[640,1024]{1,0:T(8,128)(2,1)}, bf16[640,1024]{1,0:T(8,128)(2,1)}, u32[]{:S(2)}, u32[]{:S(2)}) collective-permute-start(bf16[640,1024]{1,0:T(8,128)(2,1)} %get-tuple-element.29), channel_id=1, source_target_pairs={{0,1},{1,0},{2,3},{3,2},{4,5},{5,4},{6,7},{7,6},{8,9},{9,8},{10,11... | collective-permute-start | bytes 3932168 | tf_op jit(solution)/shard_map/ppermute | solution.py:124
  27.1 2.5 collective-permute-start.11
  29.6 192.0 %collective-permute-start.2 = (bf16[640,2048]{1,0:T(8,128)(2,1)S(1)}, bf16[640,2048]{1,0:T(8,128)(2,1)}, u32[]{:S(2)}, u32[]{:S(2)}) collective-permute-start(bf16[640,2048]{1,0:T(8,128)(2,1)S(1)} %broadcast_select_fusion.own_ref), channel_id=1, source_target_pairs={{0,16},{1,17},{2,18},{3,19},{4,20},{5,21},{6,22},{7,23},{8,24},{9,... | collective-permute-start | bytes 7864328 | tf_op jit(solution)/shard_map/ppermute | solution.py:115
  30.9 2.6 collective-permute-start.12
  32.3 68.8 %collective-permute-start.16 = (bf16[320,512]{1,0:T(8,128)(2,1)}, bf16[320,512]{1,0:T(8,128)(2,1)}, u32[]{:S(2)}, u32[]{:S(2)}) collective-permute-start(bf16[320,512]{1,0:T(8,128)(2,1)} %dynamic-slice_select_fusion.2), channel_id=1, source_target_pairs={{0,16},{1,17},{2,18},{3,19},{4,20},{5,21},{6,22},{7,23},{8,24},{9,... | collective-permute-start | bytes 983048 | tf_op jit(solution)/shard_map/ppermute | solution.py:115
  33.5 67.9 %collective-permute-start.15 = (bf16[320,512]{1,0:T(8,128)(2,1)}, bf16[320,512]{1,0:T(8,128)(2,1)}, u32[]{:S(2)}, u32[]{:S(2)}) collective-permute-start(bf16[320,512]{1,0:T(8,128)(2,1)} %dynamic-slice_select_fusion.2), channel_id=1, source_target_pairs={{0,18},{1,19},{2,16},{3,17},{4,22},{5,23},{6,20},{7,21},{8,26},{9,... | collective-permute-start | bytes 983048 | tf_op jit(solution)/shard_map/ppermute | solution.py:115
  101.1 22.1 %collective-permute-start.14 = (bf16[320,512]{1,0:T(8,128)(2,1)}, bf16[320,512]{1,0:T(8,128)(2,1)}, u32[]{:S(2)}, u32[]{:S(2)}) collective-permute-start(bf16[320,512]{1,0:T(8,128)(2,1)} %dynamic-slice_select_fusion.2), channel_id=1, source_target_pairs={{0,2},{1,3},{2,0},{3,1},{4,6},{5,7},{6,4},{7,5},{8,10},{9,11},{10,... | collective-permute-start | bytes 983048 | tf_op jit(solution)/shard_map/ppermute | solution.py:115
  103.1 22.2 %collective-permute-start.18 = (bf16[320,512]{1,0:T(8,128)(2,1)}, bf16[320,512]{1,0:T(8,128)(2,1)}, u32[]{:S(2)}, u32[]{:S(2)}) collective-permute-start(bf16[320,512]{1,0:T(8,128)(2,1)} %broadcast_select_fusion.4.refs_3_), channel_id=1, source_target_pairs={{0,1},{1,0},{2,3},{3,2},{4,5},{5,4},{6,7},{7,6},{8,9},{9,8},{10,11... | collective-permute-start | bytes 983048 | tf_op jit(solution)/shard_map/ppermute | solution.py:124
  108.6 19.1 %collective-permute-start.4 = (bf16[320,1024]{1,0:T(8,128)(2,1)}, bf16[320,1024]{1,0:T(8,128)(2,1)}, u32[]{:S(2)}, u32[]{:S(2)}) collective-permute-start(bf16[320,1024]{1,0:T(8,128)(2,1)} %get-tuple-element.27), channel_id=1, source_target_pairs={{0,2},{1,3},{2,0},{3,1},{4,6},{5,7},{6,4},{7,5},{8,10},{9,11},{10,... | collective-permute-start | bytes 1966088 | tf_op jit(solution)/shard_map/ppermute | solution.py:115
  109.8 3.6 %collective-permute-start.13 = (f32[4,1024]{1,0:T(4,128)S(1)}, f32[4,1024]{1,0:T(4,128)S(1)}, u32[]{:S(2)}, u32[]{:S(2)}) collective-permute-start(f32[4,1024]{1,0:T(4,128)S(1)} %pad_maximum_fusion.1), channel_id=1, source_target_pairs={{0,8},{1,9},{2,10},{3,11},{4,12},{5,13},{6,14},{7,15},{8,0},{9,1},... | collective-permute-start | bytes 49160 | tf_op jit(solution)/shard_map/ppermute | solution.py:146
  113.4 5.1 %collective-permute-start.10 = (bf16[2,128,320]{2,1,0:T(8,128)(2,1)S(1)}, bf16[2,128,320]{2,1,0:T(8,128)(2,1)S(1)}, u32[]{:S(2)}, u32[]{:S(2)}) collective-permute-start(bf16[2,128,320]{2,1,0:T(8,128)(2,1)S(1)} %convolution_convert_fusion.refs_0_.refs_5_), channel_id=1, source_target_pairs={{0,16},{1,17},{2,18},{3,19},{4,20},{5,21},{6,22},{7,23},{8,24},{9,... | collective-permute-start | bytes 491528 | tf_op jit(solution)/shard_map/ppermute | solution.py:115
  118.5 0.7 copy-start.4
  119.2 29.4 %collective-permute-start.7 = (bf16[320,1024]{1,0:T(8,128)(2,1)}, bf16[320,1024]{1,0:T(8,128)(2,1)}, u32[]{:S(2)}, u32[]{:S(2)}) collective-permute-start(bf16[320,1024]{1,0:T(8,128)(2,1)} %get-tuple-element.26), channel_id=1, source_target_pairs={{2,18},{3,19},{6,22},{7,23},{10,26},{11,27},{14,30},{15,31},{16,0}... | collective-permute-start | bytes 1966088 | tf_op jit(solution)/shard_map/ppermute | solution.py:115
  123.2 26.9 %collective-permute-start.6 = (bf16[320,1024]{1,0:T(8,128)(2,1)}, bf16[320,1024]{1,0:T(8,128)(2,1)}, u32[]{:S(2)}, u32[]{:S(2)}) collective-permute-start(bf16[320,1024]{1,0:T(8,128)(2,1)} %get-tuple-element.26), channel_id=1, source_target_pairs={{2,16},{3,17},{6,20},{7,21},{10,24},{11,25},{14,28},{15,29},{16,2}... | collective-permute-start | bytes 1966088 | tf_op jit(solution)/shard_map/ppermute | solution.py:115
  125.3 29.9 %collective-permute-start.21 = (bf16[640,512]{1,0:T(8,128)(2,1)S(1)}, bf16[640,512]{1,0:T(8,128)(2,1)S(1)}, u32[]{:S(2)}, u32[]{:S(2)}) collective-permute-start(bf16[640,512]{1,0:T(8,128)(2,1)S(1)} %broadcast_select_fusion.3.refs_2_), channel_id=1, source_target_pairs={{0,18},{1,19},{4,22},{5,23},{8,26},{9,27},{12,30},{13,31},{16,2},{... | collective-permute-start | bytes 1966088 | tf_op jit(solution)/shard_map/ppermute | solution.py:115
  127.6 24.4 %copy-start.5 = (bf16[320,512]{1,0:T(8,128)(2,1)}, bf16[320,512]{1,0:T(8,128)(2,1)S(1)}, u32[]{:S(2)}) copy-start(bf16[320,512]{1,0:T(8,128)(2,1)S(1)} %broadcast_select_fusion.5.refs_2_) | copy-start | bytes 983044
  127.7 24.4 %collective-permute-start.17 = (bf16[320,512]{1,0:T(8,128)(2,1)S(1)}, bf16[320,512]{1,0:T(8,128)(2,1)S(1)}, u32[]{:S(2)}, u32[]{:S(2)}) collective-permute-start(bf16[320,512]{1,0:T(8,128)(2,1)S(1)} %broadcast_select_fusion.5.refs_2_), channel_id=1, source_target_pairs={{0,1},{1,0},{2,3},{3,2},{4,5},{5,4},{6,7},{7,6},{8,9},{9,8},{10,11... | collective-permute-start | bytes 983048 | tf_op jit(solution)/shard_map/ppermute | solution.py:124
  148.5 40.2 %collective-permute-start.20 = (bf16[640,512]{1,0:T(8,128)(2,1)S(1)}, bf16[640,512]{1,0:T(8,128)(2,1)}, u32[]{:S(2)}, u32[]{:S(2)}) collective-permute-start(bf16[640,512]{1,0:T(8,128)(2,1)S(1)} %broadcast_select_fusion.3.refs_2_), channel_id=1, source_target_pairs={{0,16},{1,17},{4,20},{5,21},{8,24},{9,25},{12,28},{13,29},{16,0},{... | collective-permute-start | bytes 1966088 | tf_op jit(solution)/shard_map/ppermute | solution.py:115
  150.0 38.7 %collective-permute-start.19 = (bf16[640,512]{1,0:T(8,128)(2,1)S(1)}, bf16[640,512]{1,0:T(8,128)(2,1)}, u32[]{:S(2)}, u32[]{:S(2)}) collective-permute-start(bf16[640,512]{1,0:T(8,128)(2,1)S(1)} %broadcast_select_fusion.3.refs_2_), channel_id=1, source_target_pairs={{0,2},{1,3},{2,0},{3,1},{4,6},{5,7},{6,4},{7,5},{8,10},{9,11},{10,... | collective-permute-start | bytes 1966088 | tf_op jit(solution)/shard_map/ppermute | solution.py:115
  152.1 3.1 %copy-start.7 = (bf16[320,512]{1,0:T(8,128)(2,1)}, bf16[320,512]{1,0:T(8,128)(2,1)S(1)}, u32[]{:S(2)}) copy-start(bf16[320,512]{1,0:T(8,128)(2,1)S(1)} %collective-permute-done.17.refs_4_) | copy-start | bytes 983044
  152.1 69.5 %collective-permute-start.9 = (bf16[320,1024]{1,0:T(8,128)(2,1)}, bf16[320,1024]{1,0:T(8,128)(2,1)}, u32[]{:S(2)}, u32[]{:S(2)}) collective-permute-start(bf16[320,1024]{1,0:T(8,128)(2,1)} %broadcast_select_fusion.1.refs_2_), channel_id=1, source_target_pairs={{0,1},{1,0},{2,3},{3,2},{4,5},{5,4},{6,7},{7,6},{8,9},{9,8},{10,11... | collective-permute-start | bytes 1966088 | tf_op jit(solution)/shard_map/ppermute | solution.py:124
  155.2 0.9 copy-start.6
  156.0 65.6 %collective-permute-start.8 = (bf16[320,1024]{1,0:T(8,128)(2,1)}, bf16[320,1024]{1,0:T(8,128)(2,1)}, u32[]{:S(2)}, u32[]{:S(2)}) collective-permute-start(bf16[320,1024]{1,0:T(8,128)(2,1)} %broadcast_select_fusion.2.refs_1_), channel_id=1, source_target_pairs={{0,1},{1,0},{2,3},{3,2},{4,5},{5,4},{6,7},{7,6},{8,9},{9,8},{10,11... | collective-permute-start | bytes 1966088 | tf_op jit(solution)/shard_map/ppermute | solution.py:124
